TPU v7x, 32 devices: a whole 2x2x4 slice. The times are simulated.
32 devices in a mesh: cls: 8 (over y, x, core), batch: 4 (over z).
Axes of the slice: x: 2, y: 2, z: 4, core: 2. Of those that a mesh axis runs over, the one named last changes fastest.
Arguments:
- features: bfloat16 [4096, 1024], P('batch'), may hold values from -6 to 6
- head_weight: bfloat16 [1024, 1024], P('cls'), may hold values from -0.1875 to 0.1875
- inliers: bfloat16 [8192, 1024], P('cls'), may hold values from -2.5 to 2.5
- outliers: bfloat16 [8192, 1024], P('cls'), may hold values from -2.5 to 2.5
- inlier_counts: int32 [8192], P('cls'), may hold values from 1 to 9
- outlier_counts: int32 [8192], P('cls'), may hold values from 1 to 9
- labels: int32 [4096], P('batch'), may hold values from 0 to 1
Outputs:
- energy: float32 [4096], P('batch')
- head_grad: float32 [1024, 1024], P('cls')
All inputs are finite; a program needn't handle non-finite values.
Results may differ from a plain program's by a relative error of at most 0.0076.
The roundings to bfloat16 on the way count: a program that leaves them out, or rounds other values in their place, can miss the bound.
Values may be sent and summed in bfloat16 or wider, within the bound.
No kernel may reach another device: no remote copies, remote signals or barrier semaphores. Data moves between devices by JAX's collectives and lax.ppermute only.
A program may use at most 64 MiB of HBM per device.

v0:
```python
import functools
import math

import jax
import jax.numpy as jnp
from jax import lax
from jax.experimental import pallas as pl
from jax.experimental.pallas import tpu as pltpu
from jax.sharding import PartitionSpec as P


beta = 2.0
BF = jnp.bfloat16
F32 = jnp.float32
SHARES = (4, 4)


def orders(bits):
    turn = len(bits) // 2
    return bits, bits[turn:] + bits[:turn]


def gather_masks(order):
    masks = [0]
    for bit in order:
        masks = masks + [mask ^ (1 << bit) for mask in masks]
    return masks


def scatter_masks(order):
    masks = [0]
    for bit in reversed(order):
        masks = [mask ^ (1 << bit) for mask in masks] + masks
    return masks


def position(me, masks, p):
    core = me & 1
    return me ^ (masks[0][p] + core * (masks[1][p] - masks[0][p]))


def cls_swap(value, n, bit_of):
    return lax.ppermute(value, "cls", [(i, i ^ (1 << bit_of[i & 1])) for i in range(n)])


def batch_swap(value, n, depth, bit_of):
    pairs = []
    for i in range(n):
        for j in range(depth):
            pairs.append((i * depth + j, i * depth + (j ^ (1 << bit_of[i & 1]))))
    return lax.ppermute(value, ("cls", "batch"), pairs)


def turn_kernel(me_ref, features_ref, turned_ref, *refs, to_masks, from_masks, rows):
    me = me_ref[0]
    *lined_refs, whole_ref = refs
    whole_ref[...] = features_ref[...].T
    for masks, ref in ((to_masks, turned_ref), (from_masks, lined_refs[0] if lined_refs else None)):
        if ref is not None:
            for p in range(len(masks[0])):
                start = pl.multiple_of(position(me, masks, p) * rows, rows)
                ref[p * rows:(p + 1) * rows, :] = whole_ref[pl.ds(start, rows), :]


def turn(features, me, to_masks, from_masks, n, lined):
    q, f = features.shape
    vmem = pl.BlockSpec(memory_space=pltpu.VMEM)
    smem = pl.BlockSpec(memory_space=pltpu.SMEM)
    count = 2 if lined else 1
    return pl.pallas_call(
        functools.partial(turn_kernel, to_masks=to_masks, from_masks=from_masks, rows=f // n),
        out_shape=[jax.ShapeDtypeStruct((f, q), BF)] * count,
        in_specs=[smem, vmem],
        out_specs=[vmem] * count,
        scratch_shapes=[pltpu.VMEM((f, q), BF)],
        compiler_params=pltpu.CompilerParams(vmem_limit_bytes=16 << 20),
        cost_estimate=pl.CostEstimate(flops=0, bytes_accessed=8 * q * f, transcendentals=0),
        name="turn",
    )(me.reshape(1), features)


def join(block_refs, weight_ref):
    rows = block_refs[0].shape[0]
    for p, block_ref in enumerate(block_refs):
        weight_ref[p * rows:(p + 1) * rows, :] = block_ref[...]


def pick(me_ref, features_ref, picked_ref, masks, first, rows):
    if masks is None:
        return features_ref[:, first * rows:first * rows + picked_ref.shape[1]]
    for p in range(picked_ref.shape[1] // rows):
        start = pl.multiple_of(position(me_ref[0], masks, first + p) * rows, rows)
        picked_ref[:, p * rows:(p + 1) * rows] = features_ref[:, pl.ds(start, rows)]
    return picked_ref[...]


def part_kernel(me_ref, features_ref, *refs, masks, first, adds):
    *block_refs, out_ref, weight_ref, picked_ref = refs
    before_ref = block_refs.pop(0) if adds else None
    join(block_refs, weight_ref)
    columns = pick(me_ref, features_ref, picked_ref, masks, first, block_refs[0].shape[0])
    total = jnp.dot(columns, weight_ref[...], preferred_element_type=F32)
    out_ref[...] = before_ref[...] + total if adds else total


def query_part(me, features, blocks, masks, first, before):
    q = features.shape[0]
    rows, d = blocks[0].shape
    depth = rows * len(blocks)
    vmem = pl.BlockSpec(memory_space=pltpu.VMEM)
    return pl.pallas_call(
        functools.partial(part_kernel, masks=masks, first=first, adds=len(before)),
        out_shape=jax.ShapeDtypeStruct((q, d), F32),
        in_specs=[pl.BlockSpec(memory_space=pltpu.SMEM)] + [vmem] * (1 + len(before) + len(blocks)),
        out_specs=vmem,
        scratch_shapes=[pltpu.VMEM((depth, d), BF), pltpu.VMEM((q, depth), BF)],
        input_output_aliases={2: 0} if before else {},
        compiler_params=pltpu.CompilerParams(vmem_limit_bytes=16 << 20),
        cost_estimate=pl.CostEstimate(flops=2 * q * depth * d, bytes_accessed=4 * q * d, transcendentals=0),
        name="part",
    )(me.reshape(1), features, *before, *blocks)


def to_rows(columns, width):
    r = columns[0].shape[0]
    lane = lax.broadcasted_iota(jnp.int32, (r, width), 1)
    mixed = jnp.broadcast_to(columns[0], (r, width))
    for i, column in enumerate(columns[1:], 1):
        mixed = jnp.where(lane == i, column, mixed)
    return mixed.T[: len(columns), :]


def score_kernel(me_ref, part_ref, features_ref, in_ref, out_ref, in_counts_ref, out_counts_ref, *refs, masks):
    *block_refs, in_weights_ref, out_weights_ref, stats_ref, weight_ref, picked_ref = refs

    @pl.when(pl.program_id(0) == 0)
    def _():
        join(block_refs, weight_ref)

    rows = block_refs[0].shape[0]
    columns = pick(me_ref, features_ref, picked_ref, masks, features_ref.shape[1] // rows - len(block_refs), rows)
    late = jnp.dot(columns, weight_ref[...], preferred_element_type=F32)
    queries = (part_ref[...] + late).astype(BF) * beta
    stats = []
    for patterns_ref, counts_ref, weights_ref in (
        (in_ref, in_counts_ref, in_weights_ref),
        (out_ref, out_counts_ref, out_weights_ref),
    ):
        scores = lax.dot_general(
            queries, patterns_ref[...], (((1,), (1,)), ((), ())), preferred_element_type=F32
        ) + jnp.log(counts_ref[...].astype(F32))
        top = jnp.max(scores, axis=1, keepdims=True)
        expon = jnp.exp(scores - top)
        weights_ref[...] = expon.astype(BF)
        stats += [top, jnp.sum(expon, axis=1, keepdims=True)]
    stats_ref[...] = to_rows(stats, 128)


def local_weights(me, masks, part, features, blocks, inliers, outliers, in_counts, out_counts):
    q, f = features.shape
    late = sum(block.shape[0] for block in blocks)
    d = inliers.shape[1]
    tile = math.gcd(q, 512)
    row = lambda i: (i, 0)
    whole = lambda i: (0, 0)
    ins, outs = inliers.shape[0], outliers.shape[0]
    return pl.pallas_call(
        functools.partial(score_kernel, masks=masks),
        out_shape=(
            jax.ShapeDtypeStruct((q, ins), BF),
            jax.ShapeDtypeStruct((q, outs), BF),
            jax.ShapeDtypeStruct((4, q), F32),
        ),
        grid=(q // tile,),
        in_specs=[
            pl.BlockSpec(memory_space=pltpu.SMEM),
            pl.BlockSpec((tile, d), row),
            pl.BlockSpec((tile, f), row),
            pl.BlockSpec((ins, d), whole),
            pl.BlockSpec((outs, d), whole),
            pl.BlockSpec((1, ins), whole),
            pl.BlockSpec((1, outs), whole),
        ] + [pl.BlockSpec(block.shape, whole) for block in blocks],
        out_specs=[
            pl.BlockSpec((tile, ins), row),
            pl.BlockSpec((tile, outs), row),
            pl.BlockSpec((4, tile), lambda i: (0, i)),
        ],
        scratch_shapes=[pltpu.VMEM((late, d), BF), pltpu.VMEM((tile, late), BF)],
        compiler_params=pltpu.CompilerParams(vmem_limit_bytes=32 << 20),
        cost_estimate=pl.CostEstimate(
            flops=2 * q * d * (ins + outs), bytes_accessed=2 * d * (ins + outs), transcendentals=q * (ins + outs)
        ),
        name="scores",
    )(me.reshape(1), part, features, inliers, outliers, in_counts, out_counts, *blocks)


def merge(mine, other):
    rows = []
    for i in (0, 2):
        top = jnp.maximum(mine[i], other[i])
        rows += [top, mine[i + 1] * jnp.exp(mine[i] - top) + other[i + 1] * jnp.exp(other[i] - top)]
    return jnp.stack(rows)


def weigh_kernel(weights_ref, patterns_ref, out_ref, *, start):
    columns = patterns_ref[:, start:start + out_ref.shape[1]]
    out_ref[...] = jnp.dot(weights_ref[...], columns, preferred_element_type=F32)


def weigh(weights, patterns, start, width):
    q, count = weights.shape
    vmem = pl.BlockSpec(memory_space=pltpu.VMEM)
    return pl.pallas_call(
        functools.partial(weigh_kernel, start=start),
        out_shape=jax.ShapeDtypeStruct((q, width), F32),
        in_specs=[vmem, vmem],
        out_specs=vmem,
        compiler_params=pltpu.CompilerParams(vmem_limit_bytes=16 << 20),
        cost_estimate=pl.CostEstimate(flops=2 * q * count * width, bytes_accessed=4 * q * width, transcendentals=0),
        name="weigh",
    )(weights, patterns)


def outer_kernel(scale_ref, in_ref, out_ref, turned_ref, grad_ref, send_ref):
    q, width = in_ref.shape
    copies = width // 128

    def wide(i):
        return jnp.concatenate([jnp.broadcast_to(scale_ref[i:i + 1, :], (128, q)).T] * copies, axis=1)

    grad = (wide(0) * in_ref[...] - wide(1) * out_ref[...]).astype(BF)
    grad_ref[...] = grad
    half = send_ref.shape[0]
    send_ref[...] = jnp.dot(turned_ref[:half, :], grad, preferred_element_type=F32).astype(BF)


def outer(scales, in_sum, out_sum, turned):
    q, width = in_sum.shape
    f = turned.shape[0]
    vmem = pl.BlockSpec(memory_space=pltpu.VMEM)
    return pl.pallas_call(
        outer_kernel,
        out_shape=(jax.ShapeDtypeStruct((q, width), BF), jax.ShapeDtypeStruct((f // 2, width), BF)),
        in_specs=[vmem] * 4,
        out_specs=(vmem, vmem),
        compiler_params=pltpu.CompilerParams(vmem_limit_bytes=16 << 20),
        cost_estimate=pl.CostEstimate(flops=q * f * width, bytes_accessed=8 * q * width, transcendentals=0),
        name="outer",
    )(scales, in_sum, out_sum, turned)


def keep_kernel(turned_ref, grad_ref, keep_ref):
    half = keep_ref.shape[0]
    keep_ref[...] = jnp.dot(turned_ref[half:, :], grad_ref[...], preferred_element_type=F32)


def outer_rest(turned, grad):
    f, q = turned.shape
    width = grad.shape[1]
    vmem = pl.BlockSpec(memory_space=pltpu.VMEM)
    return pl.pallas_call(
        keep_kernel,
        out_shape=jax.ShapeDtypeStruct((f // 2, width), F32),
        in_specs=[vmem] * 2,
        out_specs=vmem,
        compiler_params=pltpu.CompilerParams(vmem_limit_bytes=16 << 20),
        cost_estimate=pl.CostEstimate(flops=q * f * width, bytes_accessed=2 * f * width, transcendentals=0),
        name="rest",
    )(turned, grad)


def body(features, head_weight, inliers, outliers, inlier_counts, outlier_counts, labels):
    n = lax.axis_size("cls")
    depth = lax.axis_size("batch")
    me = lax.axis_index("cls")
    d = head_weight.shape[1]
    links = list(range(1, n.bit_length() - 1))
    first, second = orders(links)

    held = [head_weight]
    for bit_of in zip(first, second):
        for block in list(held):
            held.append(cls_swap(block, n, bit_of))
    swapped = []
    for block in held:
        swapped.append(cls_swap(block, n, (0, 0)))
    from_first, from_second = gather_masks(first), gather_masks(second)
    groups = [slice(0, n // 4), slice(n // 4, n // 2 - 1), slice(n // 2 - 1, n // 2)]
    from_masks = [
        [mask for group in groups for mask in masks[group] + [other ^ 1 for other in others[group]]]
        for masks, others in ((from_first, from_second), (from_second, from_first))
    ]
    to_first, to_second = scatter_masks(first), scatter_masks(second)
    to_masks = [[m ^ 1 for m in to_second] + to_first, [m ^ 1 for m in to_first] + to_second]
    rows = head_weight.shape[0]
    lined = rows % 128 != 0
    turned, *lines = turn(features, me, to_masks, from_masks, n, lined)
    read_masks = None if lined else from_masks
    columns = lines[0].T if lined else features

    sums, first_block = [], 0
    *before, last = [held[group] + swapped[group] for group in groups]
    for blocks in before:
        sums = [query_part(me, columns, blocks, read_masks, first_block, sums)]
        first_block += len(blocks)
    in_weights, out_weights, stats = local_weights(
        me, read_masks, sums[0], columns, last, inliers, outliers,
        inlier_counts.reshape(1, -1), outlier_counts.reshape(1, -1),
    )
    whole = stats
    for bit in list(range(1, n.bit_length() - 1)) + [0]:
        got = cls_swap(whole, n, (bit, bit))
        whole = merge(whole, got)
    sums = []
    widths = [share * d // 8 for share in SHARES]
    for k, width in enumerate(widths):
        pair = []
        for weights, patterns in ((in_weights, inliers), (out_weights, outliers)):
            pair.append(weigh(weights, patterns, sum(widths[:k]), width))
        sums.append(pair)
    energy = ((whole[0] + jnp.log(whole[1])) - (whole[2] + jnp.log(whole[3]))) / beta
    label_sign = 2.0 * labels.astype(F32) - 1.0
    slope = -label_sign * jax.nn.sigmoid(-label_sign * energy)
    scales = jnp.stack([
        slope * jnp.exp(stats[0] - whole[0]) / whole[1],
        slope * jnp.exp(stats[2] - whole[2]) / whole[3],
    ])

    columns = []
    for in_sum, out_sum in sums:
        grad, send = outer(scales, in_sum, out_sum, turned)
        got = cls_swap(send, n, (0, 0))
        keep = outer_rest(turned, grad)
        total = keep + got.astype(F32)
        for bit_of in zip(first, second):
            middle = total.shape[0] // 2
            sent = total[:middle].astype(BF)
            got = cls_swap(sent, n, bit_of)
            total = total[middle:] + got.astype(F32)
        for bit_of in zip(*orders(list(range(depth.bit_length() - 1)))):
            sent = total.astype(BF)
            got = batch_swap(sent, n, depth, bit_of)
            total = sent.astype(F32) + got.astype(F32)
        columns.append(total)
    return energy, jnp.concatenate(columns, axis=1)


def solution(mesh):
    placed = (
        P("batch", None),
        P("cls", None),
        P("cls", None),
        P("cls", None),
        P("cls"),
        P("cls"),
        P("batch"),
    )

    return jax.shard_map(body, mesh=mesh, in_specs=placed, out_specs=(P("batch"), P("cls", None)), check_vma=False)
```

profile of v0, /device:TPU:0, one launch (start us, length us, event | category | flops | bytes accessed | tf_op | source)
XLA Modules:
  0.0 75.0 jit_solution(4825015480449139540)
XLA Ops:
  0.6 3.0 %collective-permute-start = (bf16[128,1024]{1,0:T(8,128)(2,1)}, bf16[128,1024]{1,0:T(8,128)(2,1)S(1)}, u32[]{:S(2)}, u32[]{:S(2)}) collective-permute-start(bf16[128,1024]{1,0:T(8,128)(2,1)} %refs_0_.1), channel_id=1, source_target_pairs={{0,8},{4,20},{8,0},{12,28},{16,24},{20,4},{24,16},{28,12},{1,9},{5... | collective-permute-start | bytes 786440 | tf_op jit(solution)/shard_map/ppermute | solution.py:43
  3.7 1.5 %collective-permute-start.3 = (bf16[128,1024]{1,0:T(8,128)(2,1)}, bf16[128,1024]{1,0:T(8,128)(2,1)S(1)}, u32[]{:S(2)}, u32[]{:S(2)}) collective-permute-start(bf16[128,1024]{1,0:T(8,128)(2,1)} %refs_0_.1), channel_id=1, source_target_pairs={{0,16},{4,12},{8,24},{12,4},{16,0},{20,28},{24,8},{28,20},{1,17},{... | collective-permute-start | bytes 786440 | tf_op jit(solution)/shard_map/ppermute | solution.py:43
  5.2 5.4 %collective-permute-done.refs_1_ = bf16[128,1024]{1,0:T(8,128)(2,1)S(1)} collective-permute-done((bf16[128,1024]{1,0:T(8,128)(2,1)}, bf16[128,1024]{1,0:T(8,128)(2,1)S(1)}, u32[]{:S(2)}, u32[]{:S(2)}) %collective-permute-start) | collective-permute-done | bytes 262176 | tf_op jit(solution)/shard_map/ppermute | solution.py:43
  10.6 1.5 %collective-permute-start.5 = (bf16[128,1024]{1,0:T(8,128)(2,1)S(1)}, bf16[128,1024]{1,0:T(8,128)(2,1)S(1)}, u32[]{:S(2)}, u32[]{:S(2)}) collective-permute-start(bf16[128,1024]{1,0:T(8,128)(2,1)S(1)} %collective-permute-done.refs_1_), channel_id=1, source_target_pairs={{0,16},{4,12},{8,24},{12,4},{16,0},{20,28},{24,8},{28,20},{1,17},{... | collective-permute-start | bytes 786440 | tf_op jit(solution)/shard_map/ppermute | solution.py:43
  12.0 0.5 collective-permute-start.2
  12.5 4.4 %collective-permute-done.5.refs_0_ = bf16[128,1024]{1,0:T(8,128)(2,1)S(1)} collective-permute-done((bf16[128,1024]{1,0:T(8,128)(2,1)S(1)}, bf16[128,1024]{1,0:T(8,128)(2,1)S(1)}, u32[]{:S(2)}, u32[]{:S(2)}) %collective-permute-start.5) | collective-permute-done | bytes 262176 | tf_op jit(solution)/shard_map/ppermute | solution.py:43
  17.0 1.6 %copy-done = bf16[1024,1024]{1,0:T(8,128)(2,1)S(1)} copy-done((bf16[1024,1024]{1,0:T(8,128)(2,1)S(1)}, bf16[1024,1024]{1,0:T(8,128)(2,1)}, u32[]{:S(2)}) %copy-start) | copy-done | bytes 2097176
  18.6 0.9 %copy-done.4 = bf16[128,1024]{1,0:T(8,128)(2,1)S(1)} copy-done((bf16[128,1024]{1,0:T(8,128)(2,1)S(1)}, bf16[128,1024]{1,0:T(8,128)(2,1)}, u32[]{:S(2)}) %copy-start.4) | copy-done | bytes 262168
  19.5 1.3 %part.2.refs_0_ = f32[1024,1024]{1,0:T(8,128)S(1)} custom-call(s32[1]{0:T(128)} %bitcast.me_ref, bf16[1024,1024]{1,0:T(8,128)(2,1)S(1)} %copy-done, bf16[128,1024]{1,0:T(8,128)(2,1)S(1)} %copy-done.4, bf16[128,1024]{1,0:T(8,128)(2,1)S(1)} %collective-permute-done.refs_1_, bf16[128,1024]{1,0:T(8,128)(2,1)S(1)} %collective-permute-done.1.refs_2_, ...), custom_call_target="tpu_custom_call" | custom-call | flops 1073741824 | bytes 4194304 | tf_op jit(solution)/shard_map/part/pallas_call | solution.py:111
  20.9 0.9 %part.3.part_ref = f32[1024,1024]{1,0:T(8,128)S(1)} custom-call(s32[1]{0:T(128)} %bitcast.me_ref, bf16[1024,1024]{1,0:T(8,128)(2,1)S(1)} %copy-done, f32[1024,1024]{1,0:T(8,128)S(1)} %part.2.refs_0_, bf16[128,1024]{1,0:T(8,128)(2,1)S(1)} %collective-permute-done.3.refs_1_, ...), custom_call_target="tpu_custom_call", output_to_operand_aliasing={{}: (2, {})} | custom-call | flops 536870912 | bytes 4194304 | tf_op jit(solution)/shard_map/part/pallas_call | solution.py:111
  21.8 0.7 copy-done.1
  22.4 0.6 copy-done.2
  23.0 0.6 copy-done.3
  23.7 6.8 %scores.1 = (bf16[1024,1024]{1,0:T(8,128)(2,1)S(1)}, bf16[1024,1024]{1,0:T(8,128)(2,1)S(1)}, f32[4,1024]{1,0:T(4,128)S(1)}) custom-call(s32[1]{0:T(128)} %bitcast.me_ref, f32[1024,1024]{1,0:T(8,128)S(1)} %part.3.part_ref, bf16[1024,1024]{1,0:T(8,128)(2,1)S(1)} %copy-done.1, bf16[1024,1024]{1,0:T(8,128)(2,1)S(1)} %copy-done.2, ...), custom_call_target="tpu_custom_call" | custom-call | flops 4294967296 | bytes 4194304 | tf_op jit(solution)/shard_map/scores/pallas_call | solution.py:167
  30.5 2.4 %collective-permute-start.7 = (f32[4,1024]{1,0:T(4,128)S(1)}, f32[4,1024]{1,0:T(4,128)S(1)}, u32[]{:S(2)}, u32[]{:S(2)}) collective-permute-start(f32[4,1024]{1,0:T(4,128)S(1)} %get-tuple-element.9), channel_id=1, source_target_pairs={{0,8},{4,12},{8,0},{12,4},{16,24},{20,28},{24,16},{28,20},{1,9},{5... | collective-permute-start | bytes 49160 | tf_op jit(solution)/shard_map/ppermute | solution.py:43
  33.0 0.8 %turn.1.turned_ref = bf16[1024,1024]{1,0:T(8,128)(2,1)S(1)} custom-call(s32[1]{0:T(128)} %bitcast.me_ref, bf16[1024,1024]{1,0:T(8,128)(2,1)S(1)} %copy-done.1), custom_call_target="tpu_custom_call" | custom-call | bytes 8388608 | tf_op jit(solution)/shard_map/turn/pallas_call | solution.py:70
  33.7 0.9 %collective-permute-done.7 = f32[4,1024]{1,0:T(4,128)S(1)} collective-permute-done((f32[4,1024]{1,0:T(4,128)S(1)}, f32[4,1024]{1,0:T(4,128)S(1)}, u32[]{:S(2)}, u32[]{:S(2)}) %collective-permute-start.7) | collective-permute-done | bytes 16416 | tf_op jit(solution)/shard_map/ppermute | solution.py:43
  34.8 1.2 %collective-permute-start.8 = (f32[4,1024]{1,0:T(4,128)S(1)}, f32[4,1024]{1,0:T(4,128)S(1)}, u32[]{:S(2)}, u32[]{:S(2)}) collective-permute-start(f32[4,1024]{1,0:T(4,128)S(1)} %pad_maximum_fusion.1), channel_id=1, source_target_pairs={{0,16},{4,20},{8,24},{12,28},{16,0},{20,4},{24,8},{28,12},{1,17},{... | collective-permute-start | bytes 49160 | tf_op jit(solution)/shard_map/ppermute | solution.py:43
  35.9 1.2 %weigh.4.in_ref = f32[1024,512]{1,0:T(8,128)S(1)} custom-call(bf16[1024,1024]{1,0:T(8,128)(2,1)S(1)} %get-tuple-element.10.weights_ref, bf16[1024,1024]{1,0:T(8,128)(2,1)S(1)} %copy-done.2), custom_call_target="tpu_custom_call" | custom-call | flops 1073741824 | bytes 2097152 | tf_op jit(solution)/shard_map/weigh/pallas_call | solution.py:214
  37.2 1.4 %collective-permute-done.8 = f32[4,1024]{1,0:T(4,128)S(1)} collective-permute-done((f32[4,1024]{1,0:T(4,128)S(1)}, f32[4,1024]{1,0:T(4,128)S(1)}, u32[]{:S(2)}, u32[]{:S(2)}) %collective-permute-start.8) | collective-permute-done | bytes 16416 | tf_op jit(solution)/shard_map/ppermute | solution.py:43
  38.6 0.1 collective-permute-start.9
  38.7 1.2 %weigh.5.out_ref = f32[1024,512]{1,0:T(8,128)S(1)} custom-call(bf16[1024,1024]{1,0:T(8,128)(2,1)S(1)} %get-tuple-element.11.weights_ref, bf16[1024,1024]{1,0:T(8,128)(2,1)S(1)} %copy-done.3), custom_call_target="tpu_custom_call" | custom-call | flops 1073741824 | bytes 2097152 | tf_op jit(solution)/shard_map/weigh/pallas_call | solution.py:214
  40.1 0.9 %outer.2 = (bf16[1024,512]{1,0:T(8,128)(2,1)S(1)}, bf16[512,512]{1,0:T(8,128)(2,1)S(1)}) custom-call(f32[2,1024]{1,0:T(2,128)S(1)} %pad_maximum_fusion.3.scale_ref, f32[1024,512]{1,0:T(8,128)S(1)} %weigh.4.in_ref, f32[1024,512]{1,0:T(8,128)S(1)} %weigh.5.out_ref, bf16[1024,1024]{1,0:T(8,128)(2,1)S(1)} %turn.1.turned_ref), custom_call_target="tpu_custom_call" | custom-call | flops 536870912 | bytes 4194304 | tf_op jit(solution)/shard_map/outer/pallas_call | solution.py:242
  41.0 0.6 collective-permute-start.10
  41.6 1.3 %weigh.6.in_ref = f32[1024,512]{1,0:T(8,128)S(1)} custom-call(bf16[1024,1024]{1,0:T(8,128)(2,1)S(1)} %get-tuple-element.10.weights_ref, bf16[1024,1024]{1,0:T(8,128)(2,1)S(1)} %copy-done.2), custom_call_target="tpu_custom_call" | custom-call | flops 1073741824 | bytes 2097152 | tf_op jit(solution)/shard_map/weigh/pallas_call | solution.py:214
  42.8 1.3 %weigh.7.out_ref = f32[1024,512]{1,0:T(8,128)S(1)} custom-call(bf16[1024,1024]{1,0:T(8,128)(2,1)S(1)} %get-tuple-element.11.weights_ref, bf16[1024,1024]{1,0:T(8,128)(2,1)S(1)} %copy-done.3), custom_call_target="tpu_custom_call" | custom-call | flops 1073741824 | bytes 2097152 | tf_op jit(solution)/shard_map/weigh/pallas_call | solution.py:214
  44.1 0.9 %outer.3 = (bf16[1024,512]{1,0:T(8,128)(2,1)S(1)}, bf16[512,512]{1,0:T(8,128)(2,1)S(1)}) custom-call(f32[2,1024]{1,0:T(2,128)S(1)} %pad_maximum_fusion.3.scale_ref, f32[1024,512]{1,0:T(8,128)S(1)} %weigh.6.in_ref, f32[1024,512]{1,0:T(8,128)S(1)} %weigh.7.out_ref, bf16[1024,1024]{1,0:T(8,128)(2,1)S(1)} %turn.1.turned_ref), custom_call_target="tpu_custom_call" | custom-call | flops 536870912 | bytes 4194304 | tf_op jit(solution)/shard_map/outer/pallas_call | solution.py:242
  45.0 0.1 collective-permute-start.15
  45.0 0.7 rest.3
  45.7 0.7 rest.2
  46.5 0.2 convert_add_fusion.1
  46.7 2.1 %collective-permute-start.11 = (bf16[256,512]{1,0:T(8,128)(2,1)S(1)}, bf16[256,512]{1,0:T(8,128)(2,1)S(1)}, u32[]{:S(2)}, u32[]{:S(2)}) collective-permute-start(bf16[256,512]{1,0:T(8,128)(2,1)S(1)} %slice.165), channel_id=1, source_target_pairs={{0,8},{4,20},{8,0},{12,28},{16,24},{20,4},{24,16},{28,12},{1,9},{5... | collective-permute-start | bytes 786440 | tf_op jit(solution)/shard_map/ppermute | solution.py:43
  48.8 0.2 convert_add_fusion
  49.0 0.2 collective-permute-start.16
  49.2 3.9 %collective-permute-done.11 = bf16[256,512]{1,0:T(8,128)(2,1)S(1)} collective-permute-done((bf16[256,512]{1,0:T(8,128)(2,1)S(1)}, bf16[256,512]{1,0:T(8,128)(2,1)S(1)}, u32[]{:S(2)}, u32[]{:S(2)}) %collective-permute-start.11) | collective-permute-done | bytes 262176 | tf_op jit(solution)/shard_map/ppermute | solution.py:43
  53.2 1.2 %collective-permute-start.12 = (bf16[128,512]{1,0:T(8,128)(2,1)S(1)}, bf16[128,512]{1,0:T(8,128)(2,1)S(1)}, u32[]{:S(2)}, u32[]{:S(2)}) collective-permute-start(bf16[128,512]{1,0:T(8,128)(2,1)S(1)} %slice.167), channel_id=1, source_target_pairs={{0,16},{4,12},{8,24},{12,4},{16,0},{20,28},{24,8},{28,20},{1,17},{... | collective-permute-start | bytes 393224 | tf_op jit(solution)/shard_map/ppermute | solution.py:43
  54.4 1.6 %collective-permute-done.16 = bf16[256,512]{1,0:T(8,128)(2,1)S(1)} collective-permute-done((bf16[256,512]{1,0:T(8,128)(2,1)S(1)}, bf16[256,512]{1,0:T(8,128)(2,1)S(1)}, u32[]{:S(2)}, u32[]{:S(2)}) %collective-permute-start.16) | collective-permute-done | bytes 262176 | tf_op jit(solution)/shard_map/ppermute | solution.py:43
  56.2 1.5 %collective-permute-start.17 = (bf16[128,512]{1,0:T(8,128)(2,1)S(1)}, bf16[128,512]{1,0:T(8,128)(2,1)S(1)}, u32[]{:S(2)}, u32[]{:S(2)}) collective-permute-start(bf16[128,512]{1,0:T(8,128)(2,1)S(1)} %slice.166), channel_id=1, source_target_pairs={{0,16},{4,12},{8,24},{12,4},{16,0},{20,28},{24,8},{28,20},{1,17},{... | collective-permute-start | bytes 393224 | tf_op jit(solution)/shard_map/ppermute | solution.py:43
  57.6 0.6 collective-permute-done.12
  58.3 2.2 %collective-permute-start.13 = (bf16[128,512]{1,0:T(8,128)(2,1)S(1)}, bf16[128,512]{1,0:T(8,128)(2,1)S(1)}, u32[]{:S(2)}, u32[]{:S(2)}) collective-permute-start(bf16[128,512]{1,0:T(8,128)(2,1)S(1)} %fusion.1), channel_id=1, source_target_pairs={{0,1},{1,0},{2,3},{3,2},{4,6},{5,7},{6,4},{7,5},{8,9},{9,8},{10,11... | collective-permute-start | bytes 393224 | tf_op jit(solution)/shard_map/ppermute | solution.py:51
  60.5 0.7 collective-permute-done.17
  61.2 2.5 %collective-permute-start.18 = (bf16[128,512]{1,0:T(8,128)(2,1)S(1)}, bf16[128,512]{1,0:T(8,128)(2,1)S(1)}, u32[]{:S(2)}, u32[]{:S(2)}) collective-permute-start(bf16[128,512]{1,0:T(8,128)(2,1)S(1)} %fusion), channel_id=1, source_target_pairs={{0,1},{1,0},{2,3},{3,2},{4,6},{5,7},{6,4},{7,5},{8,9},{9,8},{10,11... | collective-permute-start | bytes 393224 | tf_op jit(solution)/shard_map/ppermute | solution.py:51
  63.7 0.6 collective-permute-done.13
  64.3 3.1 %collective-permute-start.14 = (bf16[128,512]{1,0:T(8,128)(2,1)S(1)}, bf16[128,512]{1,0:T(8,128)(2,1)S(1)}, u32[]{:S(2)}, u32[]{:S(2)}) collective-permute-start(bf16[128,512]{1,0:T(8,128)(2,1)S(1)} %add_convert_fusion.1), channel_id=1, source_target_pairs={{0,2},{1,3},{2,0},{3,1},{4,5},{5,4},{6,7},{7,6},{8,10},{9,11},{10,... | collective-permute-start | bytes 393224 | tf_op jit(solution)/shard_map/ppermute | solution.py:51
  67.5 0.2 collective-permute-done.18
  67.7 3.3 %collective-permute-start.19 = (bf16[128,512]{1,0:T(8,128)(2,1)S(1)}, bf16[128,512]{1,0:T(8,128)(2,1)S(1)}, u32[]{:S(2)}, u32[]{:S(2)}) collective-permute-start(bf16[128,512]{1,0:T(8,128)(2,1)S(1)} %add_convert_fusion), channel_id=1, source_target_pairs={{0,2},{1,3},{2,0},{3,1},{4,5},{5,4},{6,7},{7,6},{8,10},{9,11},{10,... | collective-permute-start | bytes 393224 | tf_op jit(solution)/shard_map/ppermute | solution.py:51
  71.1 3.0 %collective-permute-done.19 = bf16[128,512]{1,0:T(8,128)(2,1)S(1)} collective-permute-done((bf16[128,512]{1,0:T(8,128)(2,1)S(1)}, bf16[128,512]{1,0:T(8,128)(2,1)S(1)}, u32[]{:S(2)}, u32[]{:S(2)}) %collective-permute-start.19) | collective-permute-done | bytes 131104 | tf_op jit(solution)/shard_map/ppermute | solution.py:51
  74.1 0.8 %pad_maximum_fusion = f32[128,1024]{1,0:T(8,128)} fusion(f32[128,512]{1,0:T(8,128)S(1)} %convert_add_fusion.2, f32[128,512]{1,0:T(8,128)S(1)} %convert_add_fusion.3), kind=kLoop, calls=%fused_computation.6 | loop fusion | flops 131072 | bytes 1048576 | tf_op jit(solution)/shard_map/concatenate | solution.py:346
  (45 shorter events, 0.8 us)
Async XLA Ops:
  0.6 9.9 %collective-permute-start = (bf16[128,1024]{1,0:T(8,128)(2,1)}, bf16[128,1024]{1,0:T(8,128)(2,1)S(1)}, u32[]{:S(2)}, u32[]{:S(2)}) collective-permute-start(bf16[128,1024]{1,0:T(8,128)(2,1)} %refs_0_.1), channel_id=1, source_target_pairs={{0,8},{4,20},{8,0},{12,28},{16,24},{20,4},{24,16},{28,12},{1,9},{5... | collective-permute-start | bytes 786440 | tf_op jit(solution)/shard_map/ppermute | solution.py:43
  3.7 8.9 %collective-permute-start.3 = (bf16[128,1024]{1,0:T(8,128)(2,1)}, bf16[128,1024]{1,0:T(8,128)(2,1)S(1)}, u32[]{:S(2)}, u32[]{:S(2)}) collective-permute-start(bf16[128,1024]{1,0:T(8,128)(2,1)} %refs_0_.1), channel_id=1, source_target_pairs={{0,16},{4,12},{8,24},{12,4},{16,0},{20,28},{24,8},{28,20},{1,17},{... | collective-permute-start | bytes 786440 | tf_op jit(solution)/shard_map/ppermute | solution.py:43
  10.6 6.4 %collective-permute-start.5 = (bf16[128,1024]{1,0:T(8,128)(2,1)S(1)}, bf16[128,1024]{1,0:T(8,128)(2,1)S(1)}, u32[]{:S(2)}, u32[]{:S(2)}) collective-permute-start(bf16[128,1024]{1,0:T(8,128)(2,1)S(1)} %collective-permute-done.refs_1_), channel_id=1, source_target_pairs={{0,16},{4,12},{8,24},{12,4},{16,0},{20,28},{24,8},{28,20},{1,17},{... | collective-permute-start | bytes 786440 | tf_op jit(solution)/shard_map/ppermute | solution.py:43
  12.0 4.9 %collective-permute-start.1 = (bf16[128,1024]{1,0:T(8,128)(2,1)}, bf16[128,1024]{1,0:T(8,128)(2,1)S(1)}, u32[]{:S(2)}, u32[]{:S(2)}) collective-permute-start(bf16[128,1024]{1,0:T(8,128)(2,1)} %refs_0_.1), channel_id=1, source_target_pairs={{0,4},{4,0},{8,12},{12,8},{16,20},{20,16},{24,28},{28,24},{1,5},{5... | collective-permute-start | bytes 786440 | tf_op jit(solution)/shard_map/ppermute | solution.py:43
  12.0 4.9 %collective-permute-start.2 = (bf16[128,1024]{1,0:T(8,128)(2,1)S(1)}, bf16[128,1024]{1,0:T(8,128)(2,1)S(1)}, u32[]{:S(2)}, u32[]{:S(2)}) collective-permute-start(bf16[128,1024]{1,0:T(8,128)(2,1)S(1)} %collective-permute-done.refs_1_), channel_id=1, source_target_pairs={{0,4},{4,0},{8,12},{12,8},{16,20},{20,16},{24,28},{28,24},{1,5},{5... | collective-permute-start | bytes 786440 | tf_op jit(solution)/shard_map/ppermute | solution.py:43
  12.5 8.3 %collective-permute-start.4 = (bf16[128,1024]{1,0:T(8,128)(2,1)S(1)}, bf16[128,1024]{1,0:T(8,128)(2,1)S(1)}, u32[]{:S(2)}, u32[]{:S(2)}) collective-permute-start(bf16[128,1024]{1,0:T(8,128)(2,1)S(1)} %collective-permute-done.3.refs_1_), channel_id=1, source_target_pairs={{0,4},{4,0},{8,12},{12,8},{16,20},{20,16},{24,28},{28,24},{1,5},{5... | collective-permute-start | bytes 786440 | tf_op jit(solution)/shard_map/ppermute | solution.py:43
  16.9 4.8 %collective-permute-start.6 = (bf16[128,1024]{1,0:T(8,128)(2,1)S(1)}, bf16[128,1024]{1,0:T(8,128)(2,1)S(1)}, u32[]{:S(2)}, u32[]{:S(2)}) collective-permute-start(bf16[128,1024]{1,0:T(8,128)(2,1)S(1)} %collective-permute-done.5.refs_0_), channel_id=1, source_target_pairs={{0,4},{4,0},{8,12},{12,8},{16,20},{20,16},{24,28},{28,24},{1,5},{5... | collective-permute-start | bytes 786440 | tf_op jit(solution)/shard_map/ppermute | solution.py:43
  17.0 1.6 %copy-start = (bf16[1024,1024]{1,0:T(8,128)(2,1)S(1)}, bf16[1024,1024]{1,0:T(8,128)(2,1)}, u32[]{:S(2)}) copy-start(bf16[1024,1024]{1,0:T(8,128)(2,1)} %features_ref.7) | copy-start | bytes 6291460
  18.5 0.9 %copy-start.4 = (bf16[128,1024]{1,0:T(8,128)(2,1)S(1)}, bf16[128,1024]{1,0:T(8,128)(2,1)}, u32[]{:S(2)}) copy-start(bf16[128,1024]{1,0:T(8,128)(2,1)} %refs_0_.1) | copy-start | bytes 786436
  20.8 1.6 %copy-start.1 = (bf16[1024,1024]{1,0:T(8,128)(2,1)S(1)}, bf16[1024,1024]{1,0:T(8,128)(2,1)}, u32[]{:S(2)}) copy-start(bf16[1024,1024]{1,0:T(8,128)(2,1)} %features_ref.7) | copy-start | bytes 6291460
  20.8 2.2 %copy-start.2 = (bf16[1024,1024]{1,0:T(8,128)(2,1)S(1)}, bf16[1024,1024]{1,0:T(8,128)(2,1)}, u32[]{:S(2)}) copy-start(bf16[1024,1024]{1,0:T(8,128)(2,1)} %patterns_ref.6) | copy-start | bytes 6291460
  20.8 2.8 %copy-start.3 = (bf16[1024,1024]{1,0:T(8,128)(2,1)S(1)}, bf16[1024,1024]{1,0:T(8,128)(2,1)}, u32[]{:S(2)}) copy-start(bf16[1024,1024]{1,0:T(8,128)(2,1)} %patterns_ref.7) | copy-start | bytes 6291460
  20.9 2.8 %copy-start.5 = (s32[1024]{0:T(1024)S(1)}, s32[1024]{0:T(1024)}, u32[]{:S(2)}) copy-start(s32[1024]{0:T(1024)} %param.11) | copy-start | bytes 12292
  20.9 2.8 %copy-start.6 = (s32[1024]{0:T(1024)S(1)}, s32[1024]{0:T(1024)}, u32[]{:S(2)}) copy-start(s32[1024]{0:T(1024)} %param.12) | copy-start | bytes 12292
  30.5 4.2 %collective-permute-start.7 = (f32[4,1024]{1,0:T(4,128)S(1)}, f32[4,1024]{1,0:T(4,128)S(1)}, u32[]{:S(2)}, u32[]{:S(2)}) collective-permute-start(f32[4,1024]{1,0:T(4,128)S(1)} %get-tuple-element.9), channel_id=1, source_target_pairs={{0,8},{4,12},{8,0},{12,4},{16,24},{20,28},{24,16},{28,20},{1,9},{5... | collective-permute-start | bytes 49160 | tf_op jit(solution)/shard_map/ppermute | solution.py:43
  34.8 3.8 %collective-permute-start.8 = (f32[4,1024]{1,0:T(4,128)S(1)}, f32[4,1024]{1,0:T(4,128)S(1)}, u32[]{:S(2)}, u32[]{:S(2)}) collective-permute-start(f32[4,1024]{1,0:T(4,128)S(1)} %pad_maximum_fusion.1), channel_id=1, source_target_pairs={{0,16},{4,20},{8,24},{12,28},{16,0},{20,4},{24,8},{28,12},{1,17},{... | collective-permute-start | bytes 49160 | tf_op jit(solution)/shard_map/ppermute | solution.py:43
  38.6 1.3 %collective-permute-start.9 = (f32[4,1024]{1,0:T(4,128)S(1)}, f32[4,1024]{1,0:T(4,128)S(1)}, u32[]{:S(2)}, u32[]{:S(2)}) collective-permute-start(f32[4,1024]{1,0:T(4,128)S(1)} %pad_maximum_fusion.2), channel_id=1, source_target_pairs={{0,4},{4,0},{8,12},{12,8},{16,20},{20,16},{24,28},{28,24},{1,5},{5... | collective-permute-start | bytes 49160 | tf_op jit(solution)/shard_map/ppermute | solution.py:43
  38.7 1.3 %copy-start.7 = (s32[1024]{0:T(1024)S(1)}, s32[1024]{0:T(1024)}, u32[]{:S(2)}) copy-start(s32[1024]{0:T(1024)} %param.13) | copy-start | bytes 12292
  40.1 1.0 %copy-start.8 = (f32[1024]{0:T(1024)}, f32[1024]{0:T(1024)S(1)}, u32[]{:S(2)}) copy-start(f32[1024]{0:T(1024)S(1)} %get-tuple-element.17) | copy-start | bytes 12292
  41.0 5.4 %collective-permute-start.10 = (bf16[512,512]{1,0:T(8,128)(2,1)S(1)}, bf16[512,512]{1,0:T(8,128)(2,1)S(1)}, u32[]{:S(2)}, u32[]{:S(2)}) collective-permute-start(bf16[512,512]{1,0:T(8,128)(2,1)S(1)} %get-tuple-element.13), channel_id=1, source_target_pairs={{0,4},{4,0},{8,12},{12,8},{16,20},{20,16},{24,28},{28,24},{1,5},{5... | collective-permute-start | bytes 1572872 | tf_op jit(solution)/shard_map/ppermute | solution.py:43
  45.0 3.8 %collective-permute-start.15 = (bf16[512,512]{1,0:T(8,128)(2,1)S(1)}, bf16[512,512]{1,0:T(8,128)(2,1)S(1)}, u32[]{:S(2)}, u32[]{:S(2)}) collective-permute-start(bf16[512,512]{1,0:T(8,128)(2,1)S(1)} %get-tuple-element.15), channel_id=1, source_target_pairs={{0,4},{4,0},{8,12},{12,8},{16,20},{20,16},{24,28},{28,24},{1,5},{5... | collective-permute-start | bytes 1572872 | tf_op jit(solution)/shard_map/ppermute | solution.py:43
  46.7 6.4 %collective-permute-start.11 = (bf16[256,512]{1,0:T(8,128)(2,1)S(1)}, bf16[256,512]{1,0:T(8,128)(2,1)S(1)}, u32[]{:S(2)}, u32[]{:S(2)}) collective-permute-start(bf16[256,512]{1,0:T(8,128)(2,1)S(1)} %slice.165), channel_id=1, source_target_pairs={{0,8},{4,20},{8,0},{12,28},{16,24},{20,4},{24,16},{28,12},{1,9},{5... | collective-permute-start | bytes 786440 | tf_op jit(solution)/shard_map/ppermute | solution.py:43
  49.0 7.1 %collective-permute-start.16 = (bf16[256,512]{1,0:T(8,128)(2,1)S(1)}, bf16[256,512]{1,0:T(8,128)(2,1)S(1)}, u32[]{:S(2)}, u32[]{:S(2)}) collective-permute-start(bf16[256,512]{1,0:T(8,128)(2,1)S(1)} %slice.164), channel_id=1, source_target_pairs={{0,8},{4,20},{8,0},{12,28},{16,24},{20,4},{24,16},{28,12},{1,9},{5... | collective-permute-start | bytes 786440 | tf_op jit(solution)/shard_map/ppermute | solution.py:43
  53.2 5.0 %collective-permute-start.12 = (bf16[128,512]{1,0:T(8,128)(2,1)S(1)}, bf16[128,512]{1,0:T(8,128)(2,1)S(1)}, u32[]{:S(2)}, u32[]{:S(2)}) collective-permute-start(bf16[128,512]{1,0:T(8,128)(2,1)S(1)} %slice.167), channel_id=1, source_target_pairs={{0,16},{4,12},{8,24},{12,4},{16,0},{20,28},{24,8},{28,20},{1,17},{... | collective-permute-start | bytes 393224 | tf_op jit(solution)/shard_map/ppermute | solution.py:43
  56.2 5.0 %collective-permute-start.17 = (bf16[128,512]{1,0:T(8,128)(2,1)S(1)}, bf16[128,512]{1,0:T(8,128)(2,1)S(1)}, u32[]{:S(2)}, u32[]{:S(2)}) collective-permute-start(bf16[128,512]{1,0:T(8,128)(2,1)S(1)} %slice.166), channel_id=1, source_target_pairs={{0,16},{4,12},{8,24},{12,4},{16,0},{20,28},{24,8},{28,20},{1,17},{... | collective-permute-start | bytes 393224 | tf_op jit(solution)/shard_map/ppermute | solution.py:43
  58.3 6.0 %collective-permute-start.13 = (bf16[128,512]{1,0:T(8,128)(2,1)S(1)}, bf16[128,512]{1,0:T(8,128)(2,1)S(1)}, u32[]{:S(2)}, u32[]{:S(2)}) collective-permute-start(bf16[128,512]{1,0:T(8,128)(2,1)S(1)} %fusion.1), channel_id=1, source_target_pairs={{0,1},{1,0},{2,3},{3,2},{4,6},{5,7},{6,4},{7,5},{8,9},{9,8},{10,11... | collective-permute-start | bytes 393224 | tf_op jit(solution)/shard_map/ppermute | solution.py:51
  61.2 6.5 %collective-permute-start.18 = (bf16[128,512]{1,0:T(8,128)(2,1)S(1)}, bf16[128,512]{1,0:T(8,128)(2,1)S(1)}, u32[]{:S(2)}, u32[]{:S(2)}) collective-permute-start(bf16[128,512]{1,0:T(8,128)(2,1)S(1)} %fusion), channel_id=1, source_target_pairs={{0,1},{1,0},{2,3},{3,2},{4,6},{5,7},{6,4},{7,5},{8,9},{9,8},{10,11... | collective-permute-start | bytes 393224 | tf_op jit(solution)/shard_map/ppermute | solution.py:51
  64.3 6.7 %collective-permute-start.14 = (bf16[128,512]{1,0:T(8,128)(2,1)S(1)}, bf16[128,512]{1,0:T(8,128)(2,1)S(1)}, u32[]{:S(2)}, u32[]{:S(2)}) collective-permute-start(bf16[128,512]{1,0:T(8,128)(2,1)S(1)} %add_convert_fusion.1), channel_id=1, source_target_pairs={{0,2},{1,3},{2,0},{3,1},{4,5},{5,4},{6,7},{7,6},{8,10},{9,11},{10,... | collective-permute-start | bytes 393224 | tf_op jit(solution)/shard_map/ppermute | solution.py:51
  67.7 6.4 %collective-permute-start.19 = (bf16[128,512]{1,0:T(8,128)(2,1)S(1)}, bf16[128,512]{1,0:T(8,128)(2,1)S(1)}, u32[]{:S(2)}, u32[]{:S(2)}) collective-permute-start(bf16[128,512]{1,0:T(8,128)(2,1)S(1)} %add_convert_fusion), channel_id=1, source_target_pairs={{0,2},{1,3},{2,0},{3,1},{4,5},{5,4},{6,7},{7,6},{8,10},{9,11},{10,... | collective-permute-start | bytes 393224 | tf_op jit(solution)/shard_map/ppermute | solution.py:51
where the time goes:
time: 75.2 us; the launch traced here: 75 us
  starting transfers between devices  26.9 us (36%)
  waiting for transfers between devices  22.9 us (30%)
  Pallas kernels  17.9 us (24%)
  local copies, waits for them, and re-layouts  4.62 us (6%)
  other arithmetic  1.7 us (2%)
  between operations  0.95 us (1%)
    ppermute x16, waiting for transfers between devices, cls_swap(): lax.ppermute(value, 'cls', [(i, i ^ 1 << bit_of[i & 1]) for i in range(n)])  19 us
    ppermute x16, starting transfers between devices, cls_swap(): lax.ppermute(value, 'cls', [(i, i ^ 1 << bit_of[i & 1]) for i in range(n)])  15.8 us
    ppermute x4, starting transfers between devices, batch_swap(): return lax.ppermute(value, ('cls', 'batch'), pairs)  11.1 us
    pallas_call x1, Pallas kernels, local_weights(): pl.pallas_call(functools.partial(score_kernel, masks=masks), out_shape=(j...  6.82 us
    pallas_call x4, Pallas kernels, weigh(): pl.pallas_call(functools.partial(weigh_kernel, start=start), out_shape=ja...  5.02 us
    unnamed x18, local copies, waits for them, and re-layouts  4.5 us
    ppermute x4, waiting for transfers between devices, batch_swap(): return lax.ppermute(value, ('cls', 'batch'), pairs)  3.87 us
    pallas_call x2, Pallas kernels, query_part(): pl.pallas_call(functools.partial(part_kernel, masks=masks, first=first, a...  2.17 us
  transfers between devices with their start and end apart: 20, of which 11 were waited for; matrix products, arithmetic and copies ran while one was open for 1% of the time, Pallas kernels for 14%

commit v1 on v0

--- a/solution.py
+++ b/solution.py
@@ -141,14 +141,17 @@
     columns = pick(me_ref, features_ref, picked_ref, masks, features_ref.shape[1] // rows - len(block_refs), rows)
     late = jnp.dot(columns, weight_ref[...], preferred_element_type=F32)
     queries = (part_ref[...] + late).astype(BF) * beta
-    stats = []
-    for patterns_ref, counts_ref, weights_ref in (
+    sets = (
         (in_ref, in_counts_ref, in_weights_ref),
         (out_ref, out_counts_ref, out_weights_ref),
-    ):
-        scores = lax.dot_general(
-            queries, patterns_ref[...], (((1,), (1,)), ((), ())), preferred_element_type=F32
-        ) + jnp.log(counts_ref[...].astype(F32))
+    )
+    products = [
+        lax.dot_general(queries, patterns_ref[...], (((1,), (1,)), ((), ())), preferred_element_type=F32)
+        for patterns_ref, _, _ in sets
+    ]
+    stats = []
+    for product, (_, counts_ref, weights_ref) in zip(products, sets):
+        scores = product + jnp.log(counts_ref[...].astype(F32))
         top = jnp.max(scores, axis=1, keepdims=True)
         expon = jnp.exp(scores - top)
         weights_ref[...] = expon.astype(BF)

time: 75.2 us -> 75.2 us (level)
  no operation moved by 1% of the time
where the time goes in v1:
time: 75.2 us; the launch traced here: 75 us
  starting transfers between devices  26.9 us (36%)
  waiting for transfers between devices  22.9 us (30%)
  Pallas kernels  17.9 us (24%)
  local copies, waits for them, and re-layouts  4.62 us (6%)
  other arithmetic  1.7 us (2%)
  between operations  0.95 us (1%)
    ppermute x16, waiting for transfers between devices, cls_swap(): lax.ppermute(value, 'cls', [(i, i ^ 1 << bit_of[i & 1]) for i in range(n)])  19 us
    ppermute x16, starting transfers between devices, cls_swap(): lax.ppermute(value, 'cls', [(i, i ^ 1 << bit_of[i & 1]) for i in range(n)])  15.8 us
    ppermute x4, starting transfers between devices, batch_swap(): return lax.ppermute(value, ('cls', 'batch'), pairs)  11.1 us
    pallas_call x1, Pallas kernels, local_weights(): pl.pallas_call(functools.partial(score_kernel, masks=masks), out_shape=(j...  6.82 us
    pallas_call x4, Pallas kernels, weigh(): pl.pallas_call(functools.partial(weigh_kernel, start=start), out_shape=ja...  5.02 us
    unnamed x18, local copies, waits for them, and re-layouts  4.5 us
    ppermute x4, waiting for transfers between devices, batch_swap(): return lax.ppermute(value, ('cls', 'batch'), pairs)  3.87 us
    pallas_call x2, Pallas kernels, query_part(): pl.pallas_call(functools.partial(part_kernel, masks=masks, first=first, a...  2.17 us
  transfers between devices with their start and end apart: 20, of which 11 were waited for; matrix products, arithmetic and copies ran while one was open for 1% of the time, Pallas kernels for 14%

profile of v1, /device:TPU:0, one launch (start us, length us, event | category | flops | bytes accessed | tf_op | source)
XLA Modules:
  0.0 75.0 jit_solution(4825015480449139540)
XLA Ops:
  0.6 3.0 %collective-permute-start = (bf16[128,1024]{1,0:T(8,128)(2,1)}, bf16[128,1024]{1,0:T(8,128)(2,1)S(1)}, u32[]{:S(2)}, u32[]{:S(2)}) collective-permute-start(bf16[128,1024]{1,0:T(8,128)(2,1)} %refs_0_.1), channel_id=1, source_target_pairs={{0,8},{4,20},{8,0},{12,28},{16,24},{20,4},{24,16},{28,12},{1,9},{5... | collective-permute-start | bytes 786440 | tf_op jit(solution)/shard_map/ppermute | solution.py:43
  3.7 1.5 %collective-permute-start.3 = (bf16[128,1024]{1,0:T(8,128)(2,1)}, bf16[128,1024]{1,0:T(8,128)(2,1)S(1)}, u32[]{:S(2)}, u32[]{:S(2)}) collective-permute-start(bf16[128,1024]{1,0:T(8,128)(2,1)} %refs_0_.1), channel_id=1, source_target_pairs={{0,16},{4,12},{8,24},{12,4},{16,0},{20,28},{24,8},{28,20},{1,17},{... | collective-permute-start | bytes 786440 | tf_op jit(solution)/shard_map/ppermute | solution.py:43
  5.2 5.4 %collective-permute-done.refs_1_ = bf16[128,1024]{1,0:T(8,128)(2,1)S(1)} collective-permute-done((bf16[128,1024]{1,0:T(8,128)(2,1)}, bf16[128,1024]{1,0:T(8,128)(2,1)S(1)}, u32[]{:S(2)}, u32[]{:S(2)}) %collective-permute-start) | collective-permute-done | bytes 262176 | tf_op jit(solution)/shard_map/ppermute | solution.py:43
  10.6 1.5 %collective-permute-start.5 = (bf16[128,1024]{1,0:T(8,128)(2,1)S(1)}, bf16[128,1024]{1,0:T(8,128)(2,1)S(1)}, u32[]{:S(2)}, u32[]{:S(2)}) collective-permute-start(bf16[128,1024]{1,0:T(8,128)(2,1)S(1)} %collective-permute-done.refs_1_), channel_id=1, source_target_pairs={{0,16},{4,12},{8,24},{12,4},{16,0},{20,28},{24,8},{28,20},{1,17},{... | collective-permute-start | bytes 786440 | tf_op jit(solution)/shard_map/ppermute | solution.py:43
  12.0 0.5 collective-permute-start.2
  12.5 4.4 %collective-permute-done.5.refs_0_ = bf16[128,1024]{1,0:T(8,128)(2,1)S(1)} collective-permute-done((bf16[128,1024]{1,0:T(8,128)(2,1)S(1)}, bf16[128,1024]{1,0:T(8,128)(2,1)S(1)}, u32[]{:S(2)}, u32[]{:S(2)}) %collective-permute-start.5) | collective-permute-done | bytes 262176 | tf_op jit(solution)/shard_map/ppermute | solution.py:43
  17.0 1.6 %copy-done = bf16[1024,1024]{1,0:T(8,128)(2,1)S(1)} copy-done((bf16[1024,1024]{1,0:T(8,128)(2,1)S(1)}, bf16[1024,1024]{1,0:T(8,128)(2,1)}, u32[]{:S(2)}) %copy-start) | copy-done | bytes 2097176
  18.6 0.9 %copy-done.4 = bf16[128,1024]{1,0:T(8,128)(2,1)S(1)} copy-done((bf16[128,1024]{1,0:T(8,128)(2,1)S(1)}, bf16[128,1024]{1,0:T(8,128)(2,1)}, u32[]{:S(2)}) %copy-start.4) | copy-done | bytes 262168
  19.5 1.3 %part.2.refs_0_ = f32[1024,1024]{1,0:T(8,128)S(1)} custom-call(s32[1]{0:T(128)} %bitcast.me_ref, bf16[1024,1024]{1,0:T(8,128)(2,1)S(1)} %copy-done, bf16[128,1024]{1,0:T(8,128)(2,1)S(1)} %copy-done.4, bf16[128,1024]{1,0:T(8,128)(2,1)S(1)} %collective-permute-done.refs_1_, bf16[128,1024]{1,0:T(8,128)(2,1)S(1)} %collective-permute-done.1.refs_2_, ...), custom_call_target="tpu_custom_call" | custom-call | flops 1073741824 | bytes 4194304 | tf_op jit(solution)/shard_map/part/pallas_call | solution.py:111
  20.9 0.9 %part.3.part_ref = f32[1024,1024]{1,0:T(8,128)S(1)} custom-call(s32[1]{0:T(128)} %bitcast.me_ref, bf16[1024,1024]{1,0:T(8,128)(2,1)S(1)} %copy-done, f32[1024,1024]{1,0:T(8,128)S(1)} %part.2.refs_0_, bf16[128,1024]{1,0:T(8,128)(2,1)S(1)} %collective-permute-done.3.refs_1_, ...), custom_call_target="tpu_custom_call", output_to_operand_aliasing={{}: (2, {})} | custom-call | flops 536870912 | bytes 4194304 | tf_op jit(solution)/shard_map/part/pallas_call | solution.py:111
  21.8 0.7 copy-done.1
  22.4 0.6 copy-done.2
  23.0 0.6 copy-done.3
  23.7 6.8 %scores.1 = (bf16[1024,1024]{1,0:T(8,128)(2,1)S(1)}, bf16[1024,1024]{1,0:T(8,128)(2,1)S(1)}, f32[4,1024]{1,0:T(4,128)S(1)}) custom-call(s32[1]{0:T(128)} %bitcast.me_ref, f32[1024,1024]{1,0:T(8,128)S(1)} %part.3.part_ref, bf16[1024,1024]{1,0:T(8,128)(2,1)S(1)} %copy-done.1, bf16[1024,1024]{1,0:T(8,128)(2,1)S(1)} %copy-done.2, ...), custom_call_target="tpu_custom_call" | custom-call | flops 4294967296 | bytes 4194304 | tf_op jit(solution)/shard_map/scores/pallas_call | solution.py:170
  30.5 2.4 %collective-permute-start.7 = (f32[4,1024]{1,0:T(4,128)S(1)}, f32[4,1024]{1,0:T(4,128)S(1)}, u32[]{:S(2)}, u32[]{:S(2)}) collective-permute-start(f32[4,1024]{1,0:T(4,128)S(1)} %get-tuple-element.9), channel_id=1, source_target_pairs={{0,8},{4,12},{8,0},{12,4},{16,24},{20,28},{24,16},{28,20},{1,9},{5... | collective-permute-start | bytes 49160 | tf_op jit(solution)/shard_map/ppermute | solution.py:43
  33.0 0.8 %turn.1.turned_ref = bf16[1024,1024]{1,0:T(8,128)(2,1)S(1)} custom-call(s32[1]{0:T(128)} %bitcast.me_ref, bf16[1024,1024]{1,0:T(8,128)(2,1)S(1)} %copy-done.1), custom_call_target="tpu_custom_call" | custom-call | bytes 8388608 | tf_op jit(solution)/shard_map/turn/pallas_call | solution.py:70
  33.7 0.9 %collective-permute-done.7 = f32[4,1024]{1,0:T(4,128)S(1)} collective-permute-done((f32[4,1024]{1,0:T(4,128)S(1)}, f32[4,1024]{1,0:T(4,128)S(1)}, u32[]{:S(2)}, u32[]{:S(2)}) %collective-permute-start.7) | collective-permute-done | bytes 16416 | tf_op jit(solution)/shard_map/ppermute | solution.py:43
  34.8 1.2 %collective-permute-start.8 = (f32[4,1024]{1,0:T(4,128)S(1)}, f32[4,1024]{1,0:T(4,128)S(1)}, u32[]{:S(2)}, u32[]{:S(2)}) collective-permute-start(f32[4,1024]{1,0:T(4,128)S(1)} %pad_maximum_fusion.1), channel_id=1, source_target_pairs={{0,16},{4,20},{8,24},{12,28},{16,0},{20,4},{24,8},{28,12},{1,17},{... | collective-permute-start | bytes 49160 | tf_op jit(solution)/shard_map/ppermute | solution.py:43
  35.9 1.2 %weigh.4.in_ref = f32[1024,512]{1,0:T(8,128)S(1)} custom-call(bf16[1024,1024]{1,0:T(8,128)(2,1)S(1)} %get-tuple-element.10.weights_ref, bf16[1024,1024]{1,0:T(8,128)(2,1)S(1)} %copy-done.2), custom_call_target="tpu_custom_call" | custom-call | flops 1073741824 | bytes 2097152 | tf_op jit(solution)/shard_map/weigh/pallas_call | solution.py:217
  37.2 1.4 %collective-permute-done.8 = f32[4,1024]{1,0:T(4,128)S(1)} collective-permute-done((f32[4,1024]{1,0:T(4,128)S(1)}, f32[4,1024]{1,0:T(4,128)S(1)}, u32[]{:S(2)}, u32[]{:S(2)}) %collective-permute-start.8) | collective-permute-done | bytes 16416 | tf_op jit(solution)/shard_map/ppermute | solution.py:43
  38.6 0.1 collective-permute-start.9
  38.7 1.2 %weigh.5.out_ref = f32[1024,512]{1,0:T(8,128)S(1)} custom-call(bf16[1024,1024]{1,0:T(8,128)(2,1)S(1)} %get-tuple-element.11.weights_ref, bf16[1024,1024]{1,0:T(8,128)(2,1)S(1)} %copy-done.3), custom_call_target="tpu_custom_call" | custom-call | flops 1073741824 | bytes 2097152 | tf_op jit(solution)/shard_map/weigh/pallas_call | solution.py:217
  40.1 0.9 %outer.2 = (bf16[1024,512]{1,0:T(8,128)(2,1)S(1)}, bf16[512,512]{1,0:T(8,128)(2,1)S(1)}) custom-call(f32[2,1024]{1,0:T(2,128)S(1)} %pad_maximum_fusion.3.scale_ref, f32[1024,512]{1,0:T(8,128)S(1)} %weigh.4.in_ref, f32[1024,512]{1,0:T(8,128)S(1)} %weigh.5.out_ref, bf16[1024,1024]{1,0:T(8,128)(2,1)S(1)} %turn.1.turned_ref), custom_call_target="tpu_custom_call" | custom-call | flops 536870912 | bytes 4194304 | tf_op jit(solution)/shard_map/outer/pallas_call | solution.py:245
  41.0 0.6 collective-permute-start.10
  41.6 1.3 %weigh.6.in_ref = f32[1024,512]{1,0:T(8,128)S(1)} custom-call(bf16[1024,1024]{1,0:T(8,128)(2,1)S(1)} %get-tuple-element.10.weights_ref, bf16[1024,1024]{1,0:T(8,128)(2,1)S(1)} %copy-done.2), custom_call_target="tpu_custom_call" | custom-call | flops 1073741824 | bytes 2097152 | tf_op jit(solution)/shard_map/weigh/pallas_call | solution.py:217
  42.8 1.3 %weigh.7.out_ref = f32[1024,512]{1,0:T(8,128)S(1)} custom-call(bf16[1024,1024]{1,0:T(8,128)(2,1)S(1)} %get-tuple-element.11.weights_ref, bf16[1024,1024]{1,0:T(8,128)(2,1)S(1)} %copy-done.3), custom_call_target="tpu_custom_call" | custom-call | flops 1073741824 | bytes 2097152 | tf_op jit(solution)/shard_map/weigh/pallas_call | solution.py:217
  44.1 0.9 %outer.3 = (bf16[1024,512]{1,0:T(8,128)(2,1)S(1)}, bf16[512,512]{1,0:T(8,128)(2,1)S(1)}) custom-call(f32[2,1024]{1,0:T(2,128)S(1)} %pad_maximum_fusion.3.scale_ref, f32[1024,512]{1,0:T(8,128)S(1)} %weigh.6.in_ref, f32[1024,512]{1,0:T(8,128)S(1)} %weigh.7.out_ref, bf16[1024,1024]{1,0:T(8,128)(2,1)S(1)} %turn.1.turned_ref), custom_call_target="tpu_custom_call" | custom-call | flops 536870912 | bytes 4194304 | tf_op jit(solution)/shard_map/outer/pallas_call | solution.py:245
  45.0 0.1 collective-permute-start.15
  45.0 0.7 rest.3
  45.7 0.7 rest.2
  46.5 0.2 convert_add_fusion.1
  46.7 2.1 %collective-permute-start.11 = (bf16[256,512]{1,0:T(8,128)(2,1)S(1)}, bf16[256,512]{1,0:T(8,128)(2,1)S(1)}, u32[]{:S(2)}, u32[]{:S(2)}) collective-permute-start(bf16[256,512]{1,0:T(8,128)(2,1)S(1)} %slice.165), channel_id=1, source_target_pairs={{0,8},{4,20},{8,0},{12,28},{16,24},{20,4},{24,16},{28,12},{1,9},{5... | collective-permute-start | bytes 786440 | tf_op jit(solution)/shard_map/ppermute | solution.py:43
  48.8 0.2 convert_add_fusion
  49.0 0.2 collective-permute-start.16
  49.2 3.9 %collective-permute-done.11 = bf16[256,512]{1,0:T(8,128)(2,1)S(1)} collective-permute-done((bf16[256,512]{1,0:T(8,128)(2,1)S(1)}, bf16[256,512]{1,0:T(8,128)(2,1)S(1)}, u32[]{:S(2)}, u32[]{:S(2)}) %collective-permute-start.11) | collective-permute-done | bytes 262176 | tf_op jit(solution)/shard_map/ppermute | solution.py:43
  53.2 1.2 %collective-permute-start.12 = (bf16[128,512]{1,0:T(8,128)(2,1)S(1)}, bf16[128,512]{1,0:T(8,128)(2,1)S(1)}, u32[]{:S(2)}, u32[]{:S(2)}) collective-permute-start(bf16[128,512]{1,0:T(8,128)(2,1)S(1)} %slice.167), channel_id=1, source_target_pairs={{0,16},{4,12},{8,24},{12,4},{16,0},{20,28},{24,8},{28,20},{1,17},{... | collective-permute-start | bytes 393224 | tf_op jit(solution)/shard_map/ppermute | solution.py:43
  54.4 1.6 %collective-permute-done.16 = bf16[256,512]{1,0:T(8,128)(2,1)S(1)} collective-permute-done((bf16[256,512]{1,0:T(8,128)(2,1)S(1)}, bf16[256,512]{1,0:T(8,128)(2,1)S(1)}, u32[]{:S(2)}, u32[]{:S(2)}) %collective-permute-start.16) | collective-permute-done | bytes 262176 | tf_op jit(solution)/shard_map/ppermute | solution.py:43
  56.2 1.5 %collective-permute-start.17 = (bf16[128,512]{1,0:T(8,128)(2,1)S(1)}, bf16[128,512]{1,0:T(8,128)(2,1)S(1)}, u32[]{:S(2)}, u32[]{:S(2)}) collective-permute-start(bf16[128,512]{1,0:T(8,128)(2,1)S(1)} %slice.166), channel_id=1, source_target_pairs={{0,16},{4,12},{8,24},{12,4},{16,0},{20,28},{24,8},{28,20},{1,17},{... | collective-permute-start | bytes 393224 | tf_op jit(solution)/shard_map/ppermute | solution.py:43
  57.6 0.6 collective-permute-done.12
  58.3 2.2 %collective-permute-start.13 = (bf16[128,512]{1,0:T(8,128)(2,1)S(1)}, bf16[128,512]{1,0:T(8,128)(2,1)S(1)}, u32[]{:S(2)}, u32[]{:S(2)}) collective-permute-start(bf16[128,512]{1,0:T(8,128)(2,1)S(1)} %fusion.1), channel_id=1, source_target_pairs={{0,1},{1,0},{2,3},{3,2},{4,6},{5,7},{6,4},{7,5},{8,9},{9,8},{10,11... | collective-permute-start | bytes 393224 | tf_op jit(solution)/shard_map/ppermute | solution.py:51
  60.5 0.7 collective-permute-done.17
  61.2 2.5 %collective-permute-start.18 = (bf16[128,512]{1,0:T(8,128)(2,1)S(1)}, bf16[128,512]{1,0:T(8,128)(2,1)S(1)}, u32[]{:S(2)}, u32[]{:S(2)}) collective-permute-start(bf16[128,512]{1,0:T(8,128)(2,1)S(1)} %fusion), channel_id=1, source_target_pairs={{0,1},{1,0},{2,3},{3,2},{4,6},{5,7},{6,4},{7,5},{8,9},{9,8},{10,11... | collective-permute-start | bytes 393224 | tf_op jit(solution)/shard_map/ppermute | solution.py:51
  63.7 0.6 collective-permute-done.13
  64.3 3.1 %collective-permute-start.14 = (bf16[128,512]{1,0:T(8,128)(2,1)S(1)}, bf16[128,512]{1,0:T(8,128)(2,1)S(1)}, u32[]{:S(2)}, u32[]{:S(2)}) collective-permute-start(bf16[128,512]{1,0:T(8,128)(2,1)S(1)} %add_convert_fusion.1), channel_id=1, source_target_pairs={{0,2},{1,3},{2,0},{3,1},{4,5},{5,4},{6,7},{7,6},{8,10},{9,11},{10,... | collective-permute-start | bytes 393224 | tf_op jit(solution)/shard_map/ppermute | solution.py:51
  67.5 0.2 collective-permute-done.18
  67.7 3.3 %collective-permute-start.19 = (bf16[128,512]{1,0:T(8,128)(2,1)S(1)}, bf16[128,512]{1,0:T(8,128)(2,1)S(1)}, u32[]{:S(2)}, u32[]{:S(2)}) collective-permute-start(bf16[128,512]{1,0:T(8,128)(2,1)S(1)} %add_convert_fusion), channel_id=1, source_target_pairs={{0,2},{1,3},{2,0},{3,1},{4,5},{5,4},{6,7},{7,6},{8,10},{9,11},{10,... | collective-permute-start | bytes 393224 | tf_op jit(solution)/shard_map/ppermute | solution.py:51
  71.1 3.0 %collective-permute-done.19 = bf16[128,512]{1,0:T(8,128)(2,1)S(1)} collective-permute-done((bf16[128,512]{1,0:T(8,128)(2,1)S(1)}, bf16[128,512]{1,0:T(8,128)(2,1)S(1)}, u32[]{:S(2)}, u32[]{:S(2)}) %collective-permute-start.19) | collective-permute-done | bytes 131104 | tf_op jit(solution)/shard_map/ppermute | solution.py:51
  74.1 0.8 %pad_maximum_fusion = f32[128,1024]{1,0:T(8,128)} fusion(f32[128,512]{1,0:T(8,128)S(1)} %convert_add_fusion.2, f32[128,512]{1,0:T(8,128)S(1)} %convert_add_fusion.3), kind=kLoop, calls=%fused_computation.6 | loop fusion | flops 131072 | bytes 1048576 | tf_op jit(solution)/shard_map/concatenate | solution.py:349
  (45 shorter events, 0.8 us)
Async XLA Ops:
  0.6 9.9 %collective-permute-start = (bf16[128,1024]{1,0:T(8,128)(2,1)}, bf16[128,1024]{1,0:T(8,128)(2,1)S(1)}, u32[]{:S(2)}, u32[]{:S(2)}) collective-permute-start(bf16[128,1024]{1,0:T(8,128)(2,1)} %refs_0_.1), channel_id=1, source_target_pairs={{0,8},{4,20},{8,0},{12,28},{16,24},{20,4},{24,16},{28,12},{1,9},{5... | collective-permute-start | bytes 786440 | tf_op jit(solution)/shard_map/ppermute | solution.py:43
  3.7 8.9 %collective-permute-start.3 = (bf16[128,1024]{1,0:T(8,128)(2,1)}, bf16[128,1024]{1,0:T(8,128)(2,1)S(1)}, u32[]{:S(2)}, u32[]{:S(2)}) collective-permute-start(bf16[128,1024]{1,0:T(8,128)(2,1)} %refs_0_.1), channel_id=1, source_target_pairs={{0,16},{4,12},{8,24},{12,4},{16,0},{20,28},{24,8},{28,20},{1,17},{... | collective-permute-start | bytes 786440 | tf_op jit(solution)/shard_map/ppermute | solution.py:43
  10.6 6.4 %collective-permute-start.5 = (bf16[128,1024]{1,0:T(8,128)(2,1)S(1)}, bf16[128,1024]{1,0:T(8,128)(2,1)S(1)}, u32[]{:S(2)}, u32[]{:S(2)}) collective-permute-start(bf16[128,1024]{1,0:T(8,128)(2,1)S(1)} %collective-permute-done.refs_1_), channel_id=1, source_target_pairs={{0,16},{4,12},{8,24},{12,4},{16,0},{20,28},{24,8},{28,20},{1,17},{... | collective-permute-start | bytes 786440 | tf_op jit(solution)/shard_map/ppermute | solution.py:43
  12.0 4.9 %collective-permute-start.1 = (bf16[128,1024]{1,0:T(8,128)(2,1)}, bf16[128,1024]{1,0:T(8,128)(2,1)S(1)}, u32[]{:S(2)}, u32[]{:S(2)}) collective-permute-start(bf16[128,1024]{1,0:T(8,128)(2,1)} %refs_0_.1), channel_id=1, source_target_pairs={{0,4},{4,0},{8,12},{12,8},{16,20},{20,16},{24,28},{28,24},{1,5},{5... | collective-permute-start | bytes 786440 | tf_op jit(solution)/shard_map/ppermute | solution.py:43
  12.0 4.9 %collective-permute-start.2 = (bf16[128,1024]{1,0:T(8,128)(2,1)S(1)}, bf16[128,1024]{1,0:T(8,128)(2,1)S(1)}, u32[]{:S(2)}, u32[]{:S(2)}) collective-permute-start(bf16[128,1024]{1,0:T(8,128)(2,1)S(1)} %collective-permute-done.refs_1_), channel_id=1, source_target_pairs={{0,4},{4,0},{8,12},{12,8},{16,20},{20,16},{24,28},{28,24},{1,5},{5... | collective-permute-start | bytes 786440 | tf_op jit(solution)/shard_map/ppermute | solution.py:43
  12.5 8.3 %collective-permute-start.4 = (bf16[128,1024]{1,0:T(8,128)(2,1)S(1)}, bf16[128,1024]{1,0:T(8,128)(2,1)S(1)}, u32[]{:S(2)}, u32[]{:S(2)}) collective-permute-start(bf16[128,1024]{1,0:T(8,128)(2,1)S(1)} %collective-permute-done.3.refs_1_), channel_id=1, source_target_pairs={{0,4},{4,0},{8,12},{12,8},{16,20},{20,16},{24,28},{28,24},{1,5},{5... | collective-permute-start | bytes 786440 | tf_op jit(solution)/shard_map/ppermute | solution.py:43
  16.9 4.8 %collective-permute-start.6 = (bf16[128,1024]{1,0:T(8,128)(2,1)S(1)}, bf16[128,1024]{1,0:T(8,128)(2,1)S(1)}, u32[]{:S(2)}, u32[]{:S(2)}) collective-permute-start(bf16[128,1024]{1,0:T(8,128)(2,1)S(1)} %collective-permute-done.5.refs_0_), channel_id=1, source_target_pairs={{0,4},{4,0},{8,12},{12,8},{16,20},{20,16},{24,28},{28,24},{1,5},{5... | collective-permute-start | bytes 786440 | tf_op jit(solution)/shard_map/ppermute | solution.py:43
  17.0 1.6 %copy-start = (bf16[1024,1024]{1,0:T(8,128)(2,1)S(1)}, bf16[1024,1024]{1,0:T(8,128)(2,1)}, u32[]{:S(2)}) copy-start(bf16[1024,1024]{1,0:T(8,128)(2,1)} %features_ref.7) | copy-start | bytes 6291460
  18.5 0.9 %copy-start.4 = (bf16[128,1024]{1,0:T(8,128)(2,1)S(1)}, bf16[128,1024]{1,0:T(8,128)(2,1)}, u32[]{:S(2)}) copy-start(bf16[128,1024]{1,0:T(8,128)(2,1)} %refs_0_.1) | copy-start | bytes 786436
  20.8 1.6 %copy-start.1 = (bf16[1024,1024]{1,0:T(8,128)(2,1)S(1)}, bf16[1024,1024]{1,0:T(8,128)(2,1)}, u32[]{:S(2)}) copy-start(bf16[1024,1024]{1,0:T(8,128)(2,1)} %features_ref.7) | copy-start | bytes 6291460
  20.8 2.2 %copy-start.2 = (bf16[1024,1024]{1,0:T(8,128)(2,1)S(1)}, bf16[1024,1024]{1,0:T(8,128)(2,1)}, u32[]{:S(2)}) copy-start(bf16[1024,1024]{1,0:T(8,128)(2,1)} %patterns_ref.6) | copy-start | bytes 6291460
  20.8 2.8 %copy-start.3 = (bf16[1024,1024]{1,0:T(8,128)(2,1)S(1)}, bf16[1024,1024]{1,0:T(8,128)(2,1)}, u32[]{:S(2)}) copy-start(bf16[1024,1024]{1,0:T(8,128)(2,1)} %patterns_ref.7) | copy-start | bytes 6291460
  20.9 2.8 %copy-start.5 = (s32[1024]{0:T(1024)S(1)}, s32[1024]{0:T(1024)}, u32[]{:S(2)}) copy-start(s32[1024]{0:T(1024)} %param.11) | copy-start | bytes 12292
  20.9 2.8 %copy-start.6 = (s32[1024]{0:T(1024)S(1)}, s32[1024]{0:T(1024)}, u32[]{:S(2)}) copy-start(s32[1024]{0:T(1024)} %param.12) | copy-start | bytes 12292
  30.5 4.2 %collective-permute-start.7 = (f32[4,1024]{1,0:T(4,128)S(1)}, f32[4,1024]{1,0:T(4,128)S(1)}, u32[]{:S(2)}, u32[]{:S(2)}) collective-permute-start(f32[4,1024]{1,0:T(4,128)S(1)} %get-tuple-element.9), channel_id=1, source_target_pairs={{0,8},{4,12},{8,0},{12,4},{16,24},{20,28},{24,16},{28,20},{1,9},{5... | collective-permute-start | bytes 49160 | tf_op jit(solution)/shard_map/ppermute | solution.py:43
  34.8 3.8 %collective-permute-start.8 = (f32[4,1024]{1,0:T(4,128)S(1)}, f32[4,1024]{1,0:T(4,128)S(1)}, u32[]{:S(2)}, u32[]{:S(2)}) collective-permute-start(f32[4,1024]{1,0:T(4,128)S(1)} %pad_maximum_fusion.1), channel_id=1, source_target_pairs={{0,16},{4,20},{8,24},{12,28},{16,0},{20,4},{24,8},{28,12},{1,17},{... | collective-permute-start | bytes 49160 | tf_op jit(solution)/shard_map/ppermute | solution.py:43
  38.6 1.3 %collective-permute-start.9 = (f32[4,1024]{1,0:T(4,128)S(1)}, f32[4,1024]{1,0:T(4,128)S(1)}, u32[]{:S(2)}, u32[]{:S(2)}) collective-permute-start(f32[4,1024]{1,0:T(4,128)S(1)} %pad_maximum_fusion.2), channel_id=1, source_target_pairs={{0,4},{4,0},{8,12},{12,8},{16,20},{20,16},{24,28},{28,24},{1,5},{5... | collective-permute-start | bytes 49160 | tf_op jit(solution)/shard_map/ppermute | solution.py:43
  38.7 1.3 %copy-start.7 = (s32[1024]{0:T(1024)S(1)}, s32[1024]{0:T(1024)}, u32[]{:S(2)}) copy-start(s32[1024]{0:T(1024)} %param.13) | copy-start | bytes 12292
  40.1 1.0 %copy-start.8 = (f32[1024]{0:T(1024)}, f32[1024]{0:T(1024)S(1)}, u32[]{:S(2)}) copy-start(f32[1024]{0:T(1024)S(1)} %get-tuple-element.17) | copy-start | bytes 12292
  41.0 5.4 %collective-permute-start.10 = (bf16[512,512]{1,0:T(8,128)(2,1)S(1)}, bf16[512,512]{1,0:T(8,128)(2,1)S(1)}, u32[]{:S(2)}, u32[]{:S(2)}) collective-permute-start(bf16[512,512]{1,0:T(8,128)(2,1)S(1)} %get-tuple-element.13), channel_id=1, source_target_pairs={{0,4},{4,0},{8,12},{12,8},{16,20},{20,16},{24,28},{28,24},{1,5},{5... | collective-permute-start | bytes 1572872 | tf_op jit(solution)/shard_map/ppermute | solution.py:43
  45.0 3.8 %collective-permute-start.15 = (bf16[512,512]{1,0:T(8,128)(2,1)S(1)}, bf16[512,512]{1,0:T(8,128)(2,1)S(1)}, u32[]{:S(2)}, u32[]{:S(2)}) collective-permute-start(bf16[512,512]{1,0:T(8,128)(2,1)S(1)} %get-tuple-element.15), channel_id=1, source_target_pairs={{0,4},{4,0},{8,12},{12,8},{16,20},{20,16},{24,28},{28,24},{1,5},{5... | collective-permute-start | bytes 1572872 | tf_op jit(solution)/shard_map/ppermute | solution.py:43
  46.7 6.4 %collective-permute-start.11 = (bf16[256,512]{1,0:T(8,128)(2,1)S(1)}, bf16[256,512]{1,0:T(8,128)(2,1)S(1)}, u32[]{:S(2)}, u32[]{:S(2)}) collective-permute-start(bf16[256,512]{1,0:T(8,128)(2,1)S(1)} %slice.165), channel_id=1, source_target_pairs={{0,8},{4,20},{8,0},{12,28},{16,24},{20,4},{24,16},{28,12},{1,9},{5... | collective-permute-start | bytes 786440 | tf_op jit(solution)/shard_map/ppermute | solution.py:43
  49.0 7.1 %collective-permute-start.16 = (bf16[256,512]{1,0:T(8,128)(2,1)S(1)}, bf16[256,512]{1,0:T(8,128)(2,1)S(1)}, u32[]{:S(2)}, u32[]{:S(2)}) collective-permute-start(bf16[256,512]{1,0:T(8,128)(2,1)S(1)} %slice.164), channel_id=1, source_target_pairs={{0,8},{4,20},{8,0},{12,28},{16,24},{20,4},{24,16},{28,12},{1,9},{5... | collective-permute-start | bytes 786440 | tf_op jit(solution)/shard_map/ppermute | solution.py:43
  53.2 5.0 %collective-permute-start.12 = (bf16[128,512]{1,0:T(8,128)(2,1)S(1)}, bf16[128,512]{1,0:T(8,128)(2,1)S(1)}, u32[]{:S(2)}, u32[]{:S(2)}) collective-permute-start(bf16[128,512]{1,0:T(8,128)(2,1)S(1)} %slice.167), channel_id=1, source_target_pairs={{0,16},{4,12},{8,24},{12,4},{16,0},{20,28},{24,8},{28,20},{1,17},{... | collective-permute-start | bytes 393224 | tf_op jit(solution)/shard_map/ppermute | solution.py:43
  56.2 5.0 %collective-permute-start.17 = (bf16[128,512]{1,0:T(8,128)(2,1)S(1)}, bf16[128,512]{1,0:T(8,128)(2,1)S(1)}, u32[]{:S(2)}, u32[]{:S(2)}) collective-permute-start(bf16[128,512]{1,0:T(8,128)(2,1)S(1)} %slice.166), channel_id=1, source_target_pairs={{0,16},{4,12},{8,24},{12,4},{16,0},{20,28},{24,8},{28,20},{1,17},{... | collective-permute-start | bytes 393224 | tf_op jit(solution)/shard_map/ppermute | solution.py:43
  58.3 6.0 %collective-permute-start.13 = (bf16[128,512]{1,0:T(8,128)(2,1)S(1)}, bf16[128,512]{1,0:T(8,128)(2,1)S(1)}, u32[]{:S(2)}, u32[]{:S(2)}) collective-permute-start(bf16[128,512]{1,0:T(8,128)(2,1)S(1)} %fusion.1), channel_id=1, source_target_pairs={{0,1},{1,0},{2,3},{3,2},{4,6},{5,7},{6,4},{7,5},{8,9},{9,8},{10,11... | collective-permute-start | bytes 393224 | tf_op jit(solution)/shard_map/ppermute | solution.py:51
  61.2 6.5 %collective-permute-start.18 = (bf16[128,512]{1,0:T(8,128)(2,1)S(1)}, bf16[128,512]{1,0:T(8,128)(2,1)S(1)}, u32[]{:S(2)}, u32[]{:S(2)}) collective-permute-start(bf16[128,512]{1,0:T(8,128)(2,1)S(1)} %fusion), channel_id=1, source_target_pairs={{0,1},{1,0},{2,3},{3,2},{4,6},{5,7},{6,4},{7,5},{8,9},{9,8},{10,11... | collective-permute-start | bytes 393224 | tf_op jit(solution)/shard_map/ppermute | solution.py:51
  64.3 6.7 %collective-permute-start.14 = (bf16[128,512]{1,0:T(8,128)(2,1)S(1)}, bf16[128,512]{1,0:T(8,128)(2,1)S(1)}, u32[]{:S(2)}, u32[]{:S(2)}) collective-permute-start(bf16[128,512]{1,0:T(8,128)(2,1)S(1)} %add_convert_fusion.1), channel_id=1, source_target_pairs={{0,2},{1,3},{2,0},{3,1},{4,5},{5,4},{6,7},{7,6},{8,10},{9,11},{10,... | collective-permute-start | bytes 393224 | tf_op jit(solution)/shard_map/ppermute | solution.py:51
  67.7 6.4 %collective-permute-start.19 = (bf16[128,512]{1,0:T(8,128)(2,1)S(1)}, bf16[128,512]{1,0:T(8,128)(2,1)S(1)}, u32[]{:S(2)}, u32[]{:S(2)}) collective-permute-start(bf16[128,512]{1,0:T(8,128)(2,1)S(1)} %add_convert_fusion), channel_id=1, source_target_pairs={{0,2},{1,3},{2,0},{3,1},{4,5},{5,4},{6,7},{7,6},{8,10},{9,11},{10,... | collective-permute-start | bytes 393224 | tf_op jit(solution)/shard_map/ppermute | solution.py:51
